TPU v7x, 32 devices: a whole 2x2x4 slice. The times are simulated.
32 devices in a mesh: gz: 4 (over y, core), xy: 8 (over z, x).
Axes of the slice: x: 2, y: 2, z: 4, core: 2. Of those that a mesh axis runs over, the one named last changes fastest.
Arguments:
- volume: bfloat16 [32, 64, 2048], P('gz', 'xy'), may hold values from -6 to 6
- backbone_weight: bfloat16 [64, 1728], replicated, may hold values from -0.15625 to 0.15625
- refine_weight: bfloat16 [64, 1728], replicated, may hold values from -0.15625 to 0.15625
- mix_weight: bfloat16 [64, 64], replicated, may hold values from -0.75 to 0.75
- tile_cot: bfloat16 [4, 8, 8, 2, 8, 8, 512], P('gz', 'xy'), may hold values from -6 to 6
- tile_slot: int32 [4, 8, 8, 2], P('gz', 'xy'), may hold values from 0 to 3
- tile_count: int32 [4, 8, 8], P('gz'), may hold values from 0 to 2, as said below
Outputs:
- volume_grad: bfloat16 [32, 64, 2048], P('gz', 'xy')
- backbone_step: float32 [64, 1728], replicated
- refine_step: float32 [64, 1728], replicated
- mix_step: float32 [64, 64], replicated
Inputs may be any that keep to these rules, and one draw needn't show every extreme that they name: `tile_count`: in every slab each owner receives exactly 8 live slots in all; some pairs of brick and owner use all 2 slots. `tile_slot`: only slots j < tile_count[g, s, d] are read.
All inputs are finite; a program needn't handle non-finite values.
Results may differ from a plain program's by a relative error of at most 0.0059.
Values may be sent and summed in bfloat16 or wider, within the bound.
A program may use at most 192 MiB of HBM per device.

v0:
```python
import functools

import jax
import jax.numpy as jnp
from jax import lax
from jax.experimental import pallas as pl
from jax.experimental.pallas import tpu as pltpu
from jax.sharding import PartitionSpec as P

EPSILON = 1e-06
F32 = jnp.float32
BF16 = jnp.bfloat16
VMEM = pl.BlockSpec(memory_space=pltpu.VMEM)


def with_rims(block, sides):
    for axis, dim in sides:
        count = lax.axis_size(axis)
        forward = [(i, i + 1) for i in range(count - 1)]
        backward = [(target, source) for source, target in forward]
        size = block.shape[dim]
        low = lax.ppermute(lax.slice_in_dim(block, size - 1, None, axis=dim), axis, forward)
        high = lax.ppermute(lax.slice_in_dim(block, 0, 1, axis=dim), axis, backward)
        block = jnp.concatenate([low, block, high], axis=dim)
    return block


def banded(blocks):
    w0, w1, w2 = blocks[:, 0], blocks[:, 1], blocks[:, 2]
    zero = jnp.zeros_like(w0)
    left = jnp.concatenate([w1, w2, zero, w0], axis=1)
    right = jnp.concatenate([w0, w1, w2, zero], axis=1)
    both = jnp.concatenate([left, right], axis=2)
    return both.reshape(-1, both.shape[2])


def forward_band(weight, channels):
    return banded(weight.reshape(channels, 9, 3, channels).transpose(1, 2, 0, 3))


def backward_band(weight, channels):
    blocks = weight.reshape(channels, 9, 3, channels).transpose(1, 2, 3, 0)
    return banded(blocks[::-1, ::-1])


def side_lanes(cells, half, period):
    pairs = cells.shape[1]
    lane = lax.broadcasted_iota(jnp.int32, cells.shape, 2)
    place = lax.broadcasted_iota(jnp.int32, cells.shape, 1) % period
    right = pltpu.roll(cells, pairs - 1, 1)
    left = pltpu.roll(cells, 1, 1)
    low = lane < half
    right = jnp.where(place == period - 1, 0.0, right)
    left = jnp.where(place == 0, 0.0, left)
    return jnp.where(low, right, left)


def fill_windows(target, source, half, period, inner):
    depth = target.shape[0]
    lanes = 2 * half
    if inner:
        target[...] = jnp.zeros_like(target)
    first, last = (1, depth - 1) if inner else (0, depth)
    for z in range(first, last):
        cells = source(z - first)
        rows = pl.ds(1, target.shape[1] - 2) if inner else pl.ds(0, target.shape[1])
        target[z, rows, :, pl.ds(0, lanes)] = cells.astype(BF16)
        target[z, rows, :, pl.ds(lanes, lanes)] = side_lanes(cells.astype(F32), half, period).astype(
            BF16
        )


def window_rows(windows, z, count, dz, dy):
    rows = windows.shape[1] - 2
    pairs, width = windows.shape[2], windows.shape[3]
    part = windows[pl.ds(z + dz, count), pl.ds(dy, rows)]
    return part.reshape(count * rows * pairs, width)


def conv_rows(windows, weight, z, count):
    parts = [window_rows(windows, z, count, dz, dy) for dz in range(3) for dy in range(3)]
    return jnp.dot(jnp.concatenate(parts, axis=1), weight[...], preferred_element_type=F32)


def outer_sums(out, base, windows, grad_turned, half):
    depth = windows.shape[0] - 2
    lanes = 2 * half
    lane = lax.broadcasted_iota(jnp.int32, (half, lanes), 1)
    held = None
    for offset in range(9):
        both = jnp.dot(
            grad_turned,
            window_rows(windows, 0, depth, offset // 3, offset % 3),
            preferred_element_type=F32,
        )
        top_near, top_far = both[:half, :lanes], both[:half, lanes:]
        far_turned = pltpu.roll(top_far, half, 1)
        near_turned = pltpu.roll(top_near, half, 1)
        first = jnp.where(lane < half, far_turned, near_turned) + both[half:, :lanes]
        third = near_turned + both[half:, lanes:]
        out[pl.ds(base + offset * half, half), :] = first.astype(BF16)
        if offset % 2 == 0:
            held = jnp.where(lane < half, third, 0.0)
        else:
            pair = held + jnp.where(lane < half, 0.0, pltpu.roll(third, half, 1))
            out[pl.ds(base + (9 + offset // 2) * half, half), :] = pair.astype(BF16)
    out[pl.ds(base + 13 * half, half), :] = held.astype(BF16)


def refine_kernel(
    period, vol, cot, wb, wr, wrt, mix2, fgrad, rsum, msum, xw, fw, pw, pre_s, gate_s, pg_s
):
    depth, rows, pairs, lanes = fgrad.shape
    half = lanes // 2
    step = 4 if depth % 4 == 0 else depth
    flat = step * rows * pairs
    fill_windows(xw, lambda z: vol[z], half, pairs, False)
    fw[...] = jnp.zeros_like(fw)
    pw[...] = jnp.zeros_like(pw)
    inner = pl.ds(1, rows)

    def put(target, z, cells):
        target[pl.ds(z + 1, step), inner, :, pl.ds(0, lanes)] = cells.astype(BF16)
        near = cells.astype(F32).reshape(step * rows, pairs, lanes)
        target[pl.ds(z + 1, step), inner, :, pl.ds(lanes, lanes)] = (
            side_lanes(near, half, period).astype(BF16).reshape(step, rows, pairs, lanes)
        )

    for z in range(0, depth, step):
        own = vol[pl.ds(z + 1, step), inner].astype(F32).reshape(flat, lanes)
        feature = (own + conv_rows(xw, wb, z, step)).astype(BF16)
        put(fw, z, feature.reshape(step, rows, pairs, lanes))
    for z in range(0, depth, step):
        pre = conv_rows(fw, wr, z, step)
        sig = jax.nn.sigmoid(pre)
        total = cot[pl.ds(z, step)].reshape(flat, lanes).astype(BF16)
        gate_s[pl.ds(z * rows * pairs, flat), :] = (pre * sig).astype(BF16)
        gated_grad = jnp.dot(total, mix2[...], preferred_element_type=F32)
        pre_grad = (gated_grad * sig * (1.0 + pre * (1.0 - sig))).astype(BF16)
        pg_s[pl.ds(z * rows * pairs, flat), :] = pre_grad
        put(pw, z, pre_grad.reshape(step, rows, pairs, lanes))
    for z in range(0, depth, step):
        total = cot[pl.ds(z, step)].reshape(flat, lanes)
        grad = total + conv_rows(pw, wrt, z, step)
        fgrad[pl.ds(z, step)] = grad.astype(BF16).reshape(step, rows, pairs, lanes)
    outer_sums(rsum, 0, fw, pg_s[...].T, half)
    cot_rows = cot[...].reshape(depth * rows * pairs, lanes).astype(BF16)
    both = jnp.dot(gate_s[...].T, cot_rows, preferred_element_type=F32)
    lane = lax.broadcasted_iota(jnp.int32, (half, lanes), 1)
    msum[...] = jnp.where(lane < half, both[:half] + pltpu.roll(both[half:], half, 1), 0.0).astype(
        BF16
    )


def backbone_kernel(vol, grad, wbt, rsum, msum, vgrad, sums, xw, gw):
    depth, rows, pairs, lanes = vgrad.shape
    half = lanes // 2
    step = 4 if depth % 4 == 0 else depth
    flat = step * rows * pairs
    fill_windows(xw, lambda z: vol[z], half, pairs, False)
    fill_windows(gw, lambda z: grad[z], half, pairs, False)
    inner = pl.ds(1, rows)
    for z in range(0, depth, step):
        own = grad[pl.ds(z + 1, step), inner].astype(F32).reshape(flat, lanes)
        out = own + conv_rows(gw, wbt, z, step)
        vgrad[pl.ds(z, step)] = out.astype(BF16).reshape(step, rows, pairs, lanes)
    own = grad[pl.ds(1, depth), inner].reshape(depth * rows * pairs, lanes)
    outer_sums(sums, 0, xw, own.T, half)
    block = rsum.shape[0]
    sums[pl.ds(block, block), :] = rsum[...]
    sums[pl.ds(2 * block, half), :] = msum[...]
    used = 2 * block + half
    if used < sums.shape[0]:
        sums[pl.ds(used, sums.shape[0] - used), :] = jnp.zeros(
            (sums.shape[0] - used, lanes), BF16
        )


def total_kernel(
    sizes, counts, n_xy, total_devices, sums, out, got, mine, gathered, send1, recv1, send2, recv2
):
    me = lax.axis_index("gz") * n_xy + lax.axis_index("xy")
    chunk = mine.shape[0]
    barrier = pltpu.get_barrier_semaphore()

    def peer(step):
        target = lax.rem(me + step, total_devices)
        return target, (lax.div(target, n_xy), lax.rem(target, n_xy))

    def greet(step, carry):
        _, where = peer(step)
        pl.semaphore_signal(barrier, inc=1, device_id=where, device_id_type=pl.DeviceIdType.MESH)
        return carry

    lax.fori_loop(1, total_devices, greet, 0)
    pl.semaphore_wait(barrier, total_devices - 1)

    def scatter(step):
        target, where = peer(step)
        return pltpu.make_async_remote_copy(
            src_ref=sums.at[pl.ds(target * chunk, chunk)],
            dst_ref=got.at[step],
            send_sem=send1.at[step],
            recv_sem=recv1.at[step],
            device_id=where,
            device_id_type=pl.DeviceIdType.MESH,
        )

    def gather(step):
        _, where = peer(step)
        return pltpu.make_async_remote_copy(
            src_ref=mine,
            dst_ref=gathered.at[step],
            send_sem=send2.at[step],
            recv_sem=recv2.at[step],
            device_id=where,
            device_id_type=pl.DeviceIdType.MESH,
        )

    def start1(step, carry):
        scatter(step).start()
        return carry

    lax.fori_loop(1, total_devices, start1, 0)

    def add(step, total):
        scatter(step).wait_recv()
        return total + got[step].astype(F32)

    own = sums[pl.ds(me * chunk, chunk), :].astype(F32)
    mine[...] = lax.fori_loop(1, total_devices, add, own).astype(BF16)

    def start2(step, carry):
        gather(step).start()
        return carry

    lax.fori_loop(1, total_devices, start2, 0)

    def end1(step, carry):
        scatter(step).wait_send()
        return carry

    lax.fori_loop(1, total_devices, end1, 0)
    out[pl.ds(me * chunk, chunk), :] = mine[...].astype(F32)

    def place(step, carry):
        gather(step).wait_recv()
        source = lax.rem(me + total_devices - step, total_devices)
        out[pl.ds(source * chunk, chunk), :] = gathered[step].astype(F32)
        return carry

    lax.fori_loop(1, total_devices, place, 0)

    def end2(step, carry):
        gather(step).wait_send()
        return carry

    lax.fori_loop(1, total_devices, end2, 0)
    base = 0
    for size, count in zip(sizes, counts):
        values = out[pl.ds(base, size), :]
        mean = jnp.sum(jnp.sum(values * values, axis=0, keepdims=True), axis=1, keepdims=True) / count
        out[pl.ds(base, size), :] = values / jnp.sqrt(mean + EPSILON)
        base += size


def unpacked(values, channels):
    near = values[: 9 * channels].reshape(9, channels, 2, channels).transpose(3, 0, 2, 1)
    far = values[9 * channels :].reshape(5, channels, 2, channels).transpose(3, 0, 2, 1)
    far = far.reshape(channels, 10, 1, channels)[:, :9]
    return jnp.concatenate([near, far], axis=2).reshape(channels, 27 * channels)


def body(volume, backbone_weight, refine_weight, mix_weight, tile_cot, tile_slot, tile_count):
    depth, rows, width = volume.shape
    channels = mix_weight.shape[0]
    edge = tile_cot.shape[4]
    owners, capacity = tile_cot.shape[2], tile_cot.shape[3]
    assert depth == edge and rows == edge
    lanes = 2 * channels
    pairs = width // lanes
    period = edge // 2
    tiles = pairs // period
    slots = owners * capacity
    n_gz, n_xy = lax.axis_size("gz"), lax.axis_size("xy")
    devices = n_gz * n_xy
    brick = (depth, rows, pairs, lanes)
    rimmed = with_rims(volume, (("gz", 0), ("xy", 1)))
    rimmed = rimmed.reshape(depth + 2, rows + 2, pairs, lanes)

    my_counts = jnp.sum(
        tile_count[0]
        * (jnp.arange(owners, dtype=jnp.int32) == lax.axis_index("xy")).astype(jnp.int32)[:, None],
        axis=0,
    )
    live = (jnp.arange(capacity, dtype=jnp.int32)[None, :] < my_counts[:, None]).reshape(slots)
    picker = (
        (tile_slot.reshape(slots)[None, :] == jnp.arange(tiles, dtype=jnp.int32)[:, None])
        & live[None, :]
    ).astype(BF16)
    cot = jnp.dot(
        picker, tile_cot.reshape(slots, edge * edge * edge * channels), preferred_element_type=F32
    )
    cot = cot.reshape(tiles, depth, rows, period, lanes).transpose(1, 2, 0, 3, 4).reshape(brick)

    mix_turned = mix_weight.T
    blank = jnp.zeros_like(mix_turned)
    mix2 = jnp.concatenate(
        [
            jnp.concatenate([mix_turned, blank], axis=1),
            jnp.concatenate([blank, mix_turned], axis=1),
        ],
        axis=0,
    )
    block = 14 * channels
    framed = (depth + 2, rows + 2, pairs, 2 * lanes)
    params = pltpu.CompilerParams(vmem_limit_bytes=56 * 1024 * 1024)
    fgrad, rsum, msum = pl.pallas_call(
        functools.partial(refine_kernel, period),
        out_shape=(
            jax.ShapeDtypeStruct(brick, BF16),
            jax.ShapeDtypeStruct((block, lanes), BF16),
            jax.ShapeDtypeStruct((channels, lanes), BF16),
        ),
        in_specs=[VMEM] * 6,
        out_specs=(VMEM,) * 3,
        scratch_shapes=[
            pltpu.VMEM(framed, BF16),
            pltpu.VMEM(framed, BF16),
            pltpu.VMEM(framed, BF16),
            pltpu.VMEM((8, lanes), F32),
            pltpu.VMEM((depth * rows * pairs, lanes), BF16),
            pltpu.VMEM((depth * rows * pairs, lanes), BF16),
        ],
        compiler_params=params,
    )(
        rimmed,
        cot,
        forward_band(backbone_weight, channels),
        forward_band(refine_weight, channels),
        backward_band(refine_weight, channels),
        mix2,
    )
    grad_rimmed = with_rims(fgrad, (("gz", 0), ("xy", 1)))
    used = 2 * block + channels
    chunk = -(-used // (devices * 16)) * 16
    vgrad, sums = pl.pallas_call(
        backbone_kernel,
        out_shape=(
            jax.ShapeDtypeStruct(brick, BF16),
            jax.ShapeDtypeStruct((devices * chunk, lanes), BF16),
        ),
        in_specs=[VMEM] * 5,
        out_specs=(VMEM,) * 2,
        scratch_shapes=[pltpu.VMEM(framed, BF16), pltpu.VMEM(framed, BF16)],
        compiler_params=params,
    )(rimmed, grad_rimmed, backward_band(backbone_weight, channels), rsum, msum)
    sizes = (block, block, channels)
    counts = (27.0 * channels * channels, 27.0 * channels * channels, 1.0 * channels * channels)
    totals = pl.pallas_call(
        functools.partial(total_kernel, sizes, counts, n_xy, devices),
        out_shape=jax.ShapeDtypeStruct((devices * chunk, lanes), F32),
        in_specs=[VMEM],
        out_specs=VMEM,
        scratch_shapes=[
            pltpu.VMEM((devices, chunk, lanes), BF16),
            pltpu.VMEM((chunk, lanes), BF16),
            pltpu.VMEM((devices, chunk, lanes), BF16),
        ]
        + [pltpu.SemaphoreType.DMA((devices,))] * 4,
        compiler_params=pltpu.CompilerParams(collective_id=0, has_side_effects=True),
    )(sums)
    return (
        vgrad.reshape(depth, rows, width),
        unpacked(totals[:block], channels),
        unpacked(totals[block : 2 * block], channels),
        totals[2 * block : used, :channels],
    )


def solution(mesh):
    in_specs = (
        P("gz", "xy", None),
        P(),
        P(),
        P(),
        P("gz", "xy", None, None, None, None, None),
        P("gz", "xy", None, None),
        P("gz", None, None),
    )
    out_specs = (P("gz", "xy", None), P(), P(), P())
    return jax.shard_map(body, mesh=mesh, in_specs=in_specs, out_specs=out_specs, check_vma=False)
```

profile of v0, /device:TPU:0, one launch (start us, length us, event | category | flops | bytes accessed | tf_op | source)
XLA Modules:
  0.0 121.2 jit_solution(4478720429782273770)
XLA Ops:
  0.6 1.4 %fusion.26 = (bf16[1,8,2048]{2,1,0:T(8,128)(2,1)}, bf16[1,8,2048]{2,1,0:T(8,128)(2,1)}) fusion(bf16[8,8,2048]{2,1,0:T(8,128)(2,1)} %param.7), kind=kLoop, calls=%fused_computation.60 | loop fusion | bytes 131072 | tf_op jit(solution)/shard_map/slice | solution.py:23
  2.0 3.0 %collective-permute-start = (bf16[1,8,2048]{2,1,0:T(8,128)(2,1)}, bf16[1,8,2048]{2,1,0:T(8,128)(2,1)}, u32[]{:S(2)}, u32[]{:S(2)}) collective-permute-start(bf16[1,8,2048]{2,1,0:T(8,128)(2,1)} %get-tuple-element.37), channel_id=1, source_target_pairs={{0,8},{8,16},{16,24},{1,9},{9,17},{17,25},{2,10},{10,18},{18,26},{... | collective-permute-start | bytes 98312 | tf_op jit(solution)/shard_map/ppermute | solution.py:22
  6.3 1.5 %reshape.92 = bf16[64,9,3,64]{3,2,1,0:T(4,128)(2,1)S(1)} reshape(bf16[64,1728]{1,0:T(8,128)(2,1)} %param.9) | data formatting | bytes 442368 | tf_op jit(solution)/shard_map/reshape | solution.py:38
  8.9 1.6 %reshape.88 = bf16[16,32768]{1,0:T(8,128)(2,1)S(1)} reshape(bf16[1,1,8,2,8,8,512]{6,5,4,3,2,1,0:T(8,128)(2,1)} %param.11) | data formatting | bytes 2097152 | tf_op jit(solution)/shard_map/reshape | solution.py:302
  13.1 1.3 %fusion.21 = (bf16[9,1,64,64]{3,1,0,2:T(2,128)(2,1)S(1)}, bf16[9,1,64,64]{3,1,0,2:T(2,128)(2,1)S(1)}, bf16[9,1,64,64]{3,1,0,2:T(2,128)(2,1)}) fusion(bf16[9,3,64,64]{3,1,0,2:T(4,128)(2,1)S(1)} %bitcast.61), kind=kLoop, calls=%fused_computation.55 | loop fusion | bytes 442368 | tf_op jit(solution)/shard_map/slice | solution.py:29
  14.5 1.4 %fusion.20 = (bf16[9,1,64,64]{2,1,0,3:T(2,128)(2,1)}, bf16[9,1,64,64]{2,1,0,3:T(2,128)(2,1)S(1)}, bf16[9,1,64,64]{2,1,0,3:T(2,128)(2,1)}) fusion(bf16[9,3,64,64]{2,1,0,3:T(4,128)(2,1)S(1)} %bitcast.62), kind=kLoop, calls=%fused_computation.54 | loop fusion | bytes 442368 | tf_op jit(solution)/shard_map/slice | solution.py:29
  15.9 2.8 %slice.128 = bf16[9,1,64,64]{2,1,0,3:T(2,128)(2,1)} reverse(bf16[9,1,64,64]{2,1,0,3:T(2,128)(2,1)S(1)} %get-tuple-element.19), dimensions={0,1} | reverse | bytes 147456 | tf_op jit(solution)/shard_map/slice | solution.py:29
  19.8 1.8 %slice.126 = bf16[9,1,64,64]{2,1,0,3:T(2,128)(2,1)S(1)} reverse(bf16[9,1,64,64]{2,1,0,3:T(2,128)(2,1)S(1)} %copy-done.1), dimensions={0,1} | reverse | bytes 147456 | tf_op jit(solution)/shard_map/slice | solution.py:29
  22.4 1.7 %slice.130 = bf16[9,1,64,64]{2,1,0,3:T(2,128)(2,1)S(1)} reverse(bf16[9,1,64,64]{2,1,0,3:T(2,128)(2,1)S(1)} %copy-done), dimensions={0,1} | reverse | bytes 147456 | tf_op jit(solution)/shard_map/slice | solution.py:29
  25.7 1.6 %fusion.4 = (bf16[9,256,128]{2,1,0:T(8,128)(2,1)}, bf16[9,256,128]{2,1,0:T(8,128)(2,1)}) fusion(bf16[9,64,64]{2,1,0:T(8,128)(2,1)S(1)} %broadcast.16, bf16[9,64,64]{2,1,0:T(8,128)(2,1)S(1)} %get-tuple-element.28, bf16[9,64,64]{2,1,0:T(8,128)(2,1)S(1)} %get-tuple-element.29, bf16[9,64,64]{2,1,0:T(8,128)(2,1)S(1)} %get-tuple-element.27, ...), kind=kLoop, calls=%fused_computation.16 | loop fusion | flops 8847360 | bytes 1695744 | tf_op jit(solution)/shard_map/concatenate | solution.py:33
  27.4 1.6 %fusion.8 = (bf16[9,256,128]{2,1,0:T(8,128)(2,1)}, bf16[9,256,128]{2,1,0:T(8,128)(2,1)}) fusion(bf16[9,64,64]{2,1,0:T(8,128)(2,1)S(1)} %broadcast.16, bf16[9,64,64]{2,1,0:T(8,128)(2,1)S(1)} %bitcast.75, bf16[9,64,64]{2,1,0:T(8,128)(2,1)S(1)} %bitcast.76, bf16[9,64,64]{2,1,0:T(8,128)(2,1)S(1)} %bitcast.77, bf16[9,64,64]{2,1,0:T(8,128)(2,1)S(1)} %get-tuple-element.46, ...), kind=kLoop, calls=%fused_computation.20 | loop fusion | flops 8847360 | bytes 1695744 | tf_op jit(solution)/shard_map/concatenate | solution.py:33
  30.8 1.3 %collective-permute-start.3 = (bf16[10,1,2048]{2,1,0:T(2,128)(2,1)S(1)}, bf16[10,1,2048]{2,1,0:T(2,128)(2,1)S(1)}, u32[]{:S(2)}, u32[]{:S(2)}) collective-permute-start(bf16[10,1,2048]{2,1,0:T(2,128)(2,1)S(1)} %get-tuple-element.33), channel_id=1, source_target_pairs={{1,0},{2,1},{3,2},{4,3},{5,4},{6,5},{7,6},{9,8},{10,9},{11,10},{12... | collective-permute-start | bytes 122888 | tf_op jit(solution)/shard_map/ppermute | solution.py:23
  32.1 5.0 %collective-permute-start.2 = (bf16[10,1,2048]{2,1,0:T(2,128)(2,1)S(1)}, bf16[10,1,2048]{2,1,0:T(2,128)(2,1)S(1)}, u32[]{:S(2)}, u32[]{:S(2)}) collective-permute-start(bf16[10,1,2048]{2,1,0:T(2,128)(2,1)S(1)} %get-tuple-element.32), channel_id=1, source_target_pairs={{0,1},{1,2},{2,3},{3,4},{4,5},{5,6},{6,7},{8,9},{9,10},{10,11},{11... | collective-permute-start | bytes 122888 | tf_op jit(solution)/shard_map/ppermute | solution.py:22
  38.8 1.3 %collective-permute-done.2 = bf16[10,1,2048]{2,1,0:T(2,128)(2,1)S(1)} collective-permute-done((bf16[10,1,2048]{2,1,0:T(2,128)(2,1)S(1)}, bf16[10,1,2048]{2,1,0:T(2,128)(2,1)S(1)}, u32[]{:S(2)}, u32[]{:S(2)}) %collective-permute-start.2) | collective-permute-done | bytes 40992 | tf_op jit(solution)/shard_map/ppermute | solution.py:22
  41.4 7.3 %shard_map.102 = (bf16[8,8,16,128]{3,2,1,0:T(8,128)(2,1)}, bf16[896,128]{1,0:T(8,128)(2,1)}, bf16[64,128]{1,0:T(8,128)(2,1)}) custom-call(bf16[10,10,16,128]{3,2,1,0:T(8,128)(2,1)} %reshape.87.vol, f32[8,8,16,128]{3,2,1,0:T(8,128)} %bitcast.70, bf16[2304,128]{1,0:T(8,128)(2,1)} %bitcast.68, bf16[2304,128]{1,0:T(8,128)(2,1)} %bitcast.67, ...), custom_call_target="tpu_custom_call" | custom-call | tf_op jit(solution)/shard_map/pallas_call | solution.py:318
  49.5 2.4 %collective-permute-start.4 = (bf16[1,8,16,128]{3,2,1,0:T(8,128)(2,1)S(1)}, bf16[1,8,16,128]{3,2,1,0:T(8,128)(2,1)S(1)}, u32[]{:S(2)}, u32[]{:S(2)}) collective-permute-start(bf16[1,8,16,128]{3,2,1,0:T(8,128)(2,1)S(1)} %get-tuple-element.35), channel_id=1, source_target_pairs={{0,8},{8,16},{16,24},{1,9},{9,17},{17,25},{2,10},{10,18},{18,26},{... | collective-permute-start | bytes 98312 | tf_op jit(solution)/shard_map/ppermute | solution.py:22
  51.9 1.3 %collective-permute-start.5 = (bf16[1,8,16,128]{3,2,1,0:T(8,128)(2,1)S(1)}, bf16[1,8,16,128]{3,2,1,0:T(8,128)(2,1)S(1)}, u32[]{:S(2)}, u32[]{:S(2)}) collective-permute-start(bf16[1,8,16,128]{3,2,1,0:T(8,128)(2,1)S(1)} %get-tuple-element.34), channel_id=1, source_target_pairs={{8,0},{16,8},{24,16},{9,1},{17,9},{25,17},{10,2},{18,10},{26,18},{... | collective-permute-start | bytes 98312 | tf_op jit(solution)/shard_map/ppermute | solution.py:23
  54.3 2.8 %collective-permute-done.5 = bf16[1,8,16,128]{3,2,1,0:T(8,128)(2,1)S(1)} collective-permute-done((bf16[1,8,16,128]{3,2,1,0:T(8,128)(2,1)S(1)}, bf16[1,8,16,128]{3,2,1,0:T(8,128)(2,1)S(1)}, u32[]{:S(2)}, u32[]{:S(2)}) %collective-permute-start.5) | collective-permute-done | bytes 32800 | tf_op jit(solution)/shard_map/ppermute | solution.py:23
  57.1 1.3 %collective-permute-start.7 = (bf16[10,1,16,128]{3,2,1,0:T(8,128)(2,1)S(1)}, bf16[10,1,16,128]{3,2,1,0:T(8,128)(2,1)S(1)}, u32[]{:S(2)}, u32[]{:S(2)}) collective-permute-start(bf16[10,1,16,128]{3,2,1,0:T(8,128)(2,1)S(1)} %get-tuple-element.31), channel_id=1, source_target_pairs={{1,0},{2,1},{3,2},{4,3},{5,4},{6,5},{7,6},{9,8},{10,9},{11,10},{12... | collective-permute-start | bytes 122888 | tf_op jit(solution)/shard_map/ppermute | solution.py:23
  58.4 5.1 %collective-permute-start.6 = (bf16[10,1,16,128]{3,2,1,0:T(8,128)(2,1)S(1)}, bf16[10,1,16,128]{3,2,1,0:T(8,128)(2,1)S(1)}, u32[]{:S(2)}, u32[]{:S(2)}) collective-permute-start(bf16[10,1,16,128]{3,2,1,0:T(8,128)(2,1)S(1)} %get-tuple-element.30), channel_id=1, source_target_pairs={{0,1},{1,2},{2,3},{3,4},{4,5},{5,6},{6,7},{8,9},{9,10},{10,11},{11... | collective-permute-start | bytes 122888 | tf_op jit(solution)/shard_map/ppermute | solution.py:22
  63.5 1.4 %collective-permute-done.6 = bf16[10,1,16,128]{3,2,1,0:T(8,128)(2,1)S(1)} collective-permute-done((bf16[10,1,16,128]{3,2,1,0:T(8,128)(2,1)S(1)}, bf16[10,1,16,128]{3,2,1,0:T(8,128)(2,1)S(1)}, u32[]{:S(2)}, u32[]{:S(2)}) %collective-permute-start.6) | collective-permute-done | bytes 40992 | tf_op jit(solution)/shard_map/ppermute | solution.py:22
  65.8 4.4 %shard_map.103 = (bf16[8,8,16,128]{3,2,1,0:T(8,128)(2,1)}, bf16[2048,128]{1,0:T(8,128)(2,1)}) custom-call(bf16[10,10,16,128]{3,2,1,0:T(8,128)(2,1)} %reshape.87.vol, bf16[10,10,16,128]{3,2,1,0:T(8,128)(2,1)} %pad_maximum_fusion.11.grad, bf16[2304,128]{1,0:T(8,128)(2,1)} %bitcast.64, bf16[896,128]{1,0:T(8,128)(2,1)} %get-tuple-element.10.rsum, ...), custom_call_target="tpu_custom_call" | custom-call | tf_op jit(solution)/shard_map/pallas_call | solution.py:347
  70.2 38.9 %shard_map.104 = f32[2048,128]{1,0:T(8,128)} custom-call(bf16[2048,128]{1,0:T(8,128)(2,1)} %get-tuple-element.13.sums), custom_call_target="tpu_custom_call" | custom-call | tf_op jit(solution)/shard_map/pallas_call | solution.py:360
  111.2 1.4 %slice.137 = f32[64,64]{1,0:T(8,128)} slice(f32[2048,128]{1,0:T(8,128)} %shard_map.104), slice={[1792:1856], [0:64]} | slice | bytes 32768 | tf_op jit(solution)/shard_map/slice | solution.py:377
  (84 shorter events, 26.4 us)
Async XLA Ops:
  2.0 27.1 %collective-permute-start = (bf16[1,8,2048]{2,1,0:T(8,128)(2,1)}, bf16[1,8,2048]{2,1,0:T(8,128)(2,1)}, u32[]{:S(2)}, u32[]{:S(2)}) collective-permute-start(bf16[1,8,2048]{2,1,0:T(8,128)(2,1)} %get-tuple-element.37), channel_id=1, source_target_pairs={{0,8},{8,16},{16,24},{1,9},{9,17},{17,25},{2,10},{10,18},{18,26},{... | collective-permute-start | bytes 98312 | tf_op jit(solution)/shard_map/ppermute | solution.py:22
  5.0 24.9 %collective-permute-start.1 = (bf16[1,8,2048]{2,1,0:T(8,128)(2,1)}, bf16[1,8,2048]{2,1,0:T(8,128)(2,1)}, u32[]{:S(2)}, u32[]{:S(2)}) collective-permute-start(bf16[1,8,2048]{2,1,0:T(8,128)(2,1)} %get-tuple-element.36), channel_id=1, source_target_pairs={{8,0},{16,8},{24,16},{9,1},{17,9},{25,17},{10,2},{18,10},{26,18},{... | collective-permute-start | bytes 98312 | tf_op jit(solution)/shard_map/ppermute | solution.py:23
  10.4 0.8 copy-start.10
  10.4 1.6 %copy-start.8 = (s32[1,8,8]{2,1,0:T(8,128)S(1)}, s32[1,8,8]{2,1,0:T(8,128)}, u32[]{:S(2)}) copy-start(s32[1,8,8]{2,1,0:T(8,128)} %param.13) | copy-start | bytes 772
  10.4 2.3 %copy-start.6 = (bf16[64,1728]{1,0:T(8,128)(2,1)S(1)}, bf16[64,1728]{1,0:T(8,128)(2,1)}, u32[]{:S(2)}) copy-start(bf16[64,1728]{1,0:T(8,128)(2,1)} %param.8) | copy-start | bytes 663556
  15.9 3.9 %copy-start.1 = (bf16[9,1,64,64]{2,1,0,3:T(2,128)(2,1)S(1)}, bf16[9,1,64,64]{2,1,0,3:T(2,128)(2,1)}, u32[]{:S(2)}) copy-start(bf16[9,1,64,64]{2,1,0,3:T(2,128)(2,1)} %get-tuple-element.20) | copy-start | bytes 221188
  15.9 6.5 %copy-start = (bf16[9,1,64,64]{2,1,0,3:T(2,128)(2,1)S(1)}, bf16[9,1,64,64]{2,1,0,3:T(2,128)(2,1)}, u32[]{:S(2)}) copy-start(bf16[9,1,64,64]{2,1,0,3:T(2,128)(2,1)} %get-tuple-element.18) | copy-start | bytes 221188
  22.4 2.0 %copy-start.2 = (bf16[9,1,64,64]{3,1,0,2:T(2,128)(2,1)S(1)}, bf16[9,1,64,64]{3,1,0,2:T(2,128)(2,1)}, u32[]{:S(2)}) copy-start(bf16[9,1,64,64]{3,1,0,2:T(2,128)(2,1)} %get-tuple-element.23) | copy-start | bytes 221188
  24.4 0.7 copy-start.9
  24.4 0.7 copy-start.11
  25.7 1.7 %copy-start.3 = (bf16[9,1,64,64]{3,2,0,1:T(8,128)(2,1)S(1)}, bf16[9,1,64,64]{3,2,0,1:T(8,128)(2,1)}, u32[]{:S(2)}) copy-start(bf16[9,1,64,64]{3,2,0,1:T(8,128)(2,1)} %copy.179) | copy-start | bytes 221188
  27.4 1.6 %copy-start.7 = (bf16[64,64]{1,0:T(8,128)(2,1)S(1)}, bf16[64,64]{1,0:T(8,128)(2,1)}, u32[]{:S(2)}) copy-start(bf16[64,64]{1,0:T(8,128)(2,1)} %param.10) | copy-start | bytes 24580
  27.4 2.5 %copy-start.4 = (bf16[8,8,2048]{2,1,0:T(8,128)(2,1)S(1)}, bf16[8,8,2048]{2,1,0:T(8,128)(2,1)}, u32[]{:S(2)}) copy-start(bf16[8,8,2048]{2,1,0:T(8,128)(2,1)} %param.7) | copy-start | bytes 786436
  30.8 8.0 %collective-permute-start.3 = (bf16[10,1,2048]{2,1,0:T(2,128)(2,1)S(1)}, bf16[10,1,2048]{2,1,0:T(2,128)(2,1)S(1)}, u32[]{:S(2)}, u32[]{:S(2)}) collective-permute-start(bf16[10,1,2048]{2,1,0:T(2,128)(2,1)S(1)} %get-tuple-element.33), channel_id=1, source_target_pairs={{1,0},{2,1},{3,2},{4,3},{5,4},{6,5},{7,6},{9,8},{10,9},{11,10},{12... | collective-permute-start | bytes 122888 | tf_op jit(solution)/shard_map/ppermute | solution.py:23
  32.1 8.0 %collective-permute-start.2 = (bf16[10,1,2048]{2,1,0:T(2,128)(2,1)S(1)}, bf16[10,1,2048]{2,1,0:T(2,128)(2,1)S(1)}, u32[]{:S(2)}, u32[]{:S(2)}) collective-permute-start(bf16[10,1,2048]{2,1,0:T(2,128)(2,1)S(1)} %get-tuple-element.32), channel_id=1, source_target_pairs={{0,1},{1,2},{2,3},{3,4},{4,5},{5,6},{6,7},{8,9},{9,10},{10,11},{11... | collective-permute-start | bytes 122888 | tf_op jit(solution)/shard_map/ppermute | solution.py:22
  49.5 3.7 %collective-permute-start.4 = (bf16[1,8,16,128]{3,2,1,0:T(8,128)(2,1)S(1)}, bf16[1,8,16,128]{3,2,1,0:T(8,128)(2,1)S(1)}, u32[]{:S(2)}, u32[]{:S(2)}) collective-permute-start(bf16[1,8,16,128]{3,2,1,0:T(8,128)(2,1)S(1)} %get-tuple-element.35), channel_id=1, source_target_pairs={{0,8},{8,16},{16,24},{1,9},{9,17},{17,25},{2,10},{10,18},{18,26},{... | collective-permute-start | bytes 98312 | tf_op jit(solution)/shard_map/ppermute | solution.py:22
  51.9 5.1 %collective-permute-start.5 = (bf16[1,8,16,128]{3,2,1,0:T(8,128)(2,1)S(1)}, bf16[1,8,16,128]{3,2,1,0:T(8,128)(2,1)S(1)}, u32[]{:S(2)}, u32[]{:S(2)}) collective-permute-start(bf16[1,8,16,128]{3,2,1,0:T(8,128)(2,1)S(1)} %get-tuple-element.34), channel_id=1, source_target_pairs={{8,0},{16,8},{24,16},{9,1},{17,9},{25,17},{10,2},{18,10},{26,18},{... | collective-permute-start | bytes 98312 | tf_op jit(solution)/shard_map/ppermute | solution.py:23
  57.1 6.5 %collective-permute-start.7 = (bf16[10,1,16,128]{3,2,1,0:T(8,128)(2,1)S(1)}, bf16[10,1,16,128]{3,2,1,0:T(8,128)(2,1)S(1)}, u32[]{:S(2)}, u32[]{:S(2)}) collective-permute-start(bf16[10,1,16,128]{3,2,1,0:T(8,128)(2,1)S(1)} %get-tuple-element.31), channel_id=1, source_target_pairs={{1,0},{2,1},{3,2},{4,3},{5,4},{6,5},{7,6},{9,8},{10,9},{11,10},{12... | collective-permute-start | bytes 122888 | tf_op jit(solution)/shard_map/ppermute | solution.py:23
  58.4 6.6 %collective-permute-start.6 = (bf16[10,1,16,128]{3,2,1,0:T(8,128)(2,1)S(1)}, bf16[10,1,16,128]{3,2,1,0:T(8,128)(2,1)S(1)}, u32[]{:S(2)}, u32[]{:S(2)}) collective-permute-start(bf16[10,1,16,128]{3,2,1,0:T(8,128)(2,1)S(1)} %get-tuple-element.30), channel_id=1, source_target_pairs={{0,1},{1,2},{2,3},{3,4},{4,5},{5,6},{6,7},{8,9},{9,10},{10,11},{11... | collective-permute-start | bytes 122888 | tf_op jit(solution)/shard_map/ppermute | solution.py:22
  109.1 3.5 %copy-start.5 = (bf16[8,8,16,128]{3,2,1,0:T(8,128)(2,1)S(1)}, bf16[8,8,16,128]{3,2,1,0:T(8,128)(2,1)}, u32[]{:S(2)}) copy-start(bf16[8,8,16,128]{3,2,1,0:T(8,128)(2,1)} %get-tuple-element.12) | copy-start | bytes 786436
where the time goes:
time: 122 us; the launch traced here: 121 us
  Pallas kernels  50.6 us (41%)
  local copies, waits for them, and re-layouts  36.1 us (30%)
  starting transfers between devices  20.7 us (17%)
  other arithmetic  6.55 us (5%)
  waiting for transfers between devices  5.55 us (5%)
    pallas_call x1, Pallas kernels, body(): pl.pallas_call(functools.partial(total_kernel, sizes, counts, n_xy, devic...  38.9 us
    ppermute x4, starting transfers between devices, with_rims(): lax.ppermute(lax.slice_in_dim(block, size - 1, None, axis=dim), axis, for...  15.6 us
    slice x9, local copies, waits for them, and re-layouts, banded(): w0, w1, w2 = (blocks[:, 0], blocks[:, 1], blocks[:, 2])  11.2 us
    pallas_call x1, Pallas kernels, body(): pl.pallas_call(functools.partial(refine_kernel, period), out_shape=(jax.S...  7.33 us
    ppermute x4, starting transfers between devices, with_rims(): high = lax.ppermute(lax.slice_in_dim(block, 0, 1, axis=dim), axis, backward)  5.16 us
    pallas_call x1, Pallas kernels, body(): pl.pallas_call(backbone_kernel, out_shape=(jax.ShapeDtypeStruct(brick, BF...  4.43 us
    concatenate x2, other arithmetic, banded(): both = jnp.concatenate([left, right], axis=2)  3.27 us
    reshape x4, local copies, waits for them, and re-layouts, forward_band(): weight.reshape(channels, 9, 3, channels).transpose(1, 2, 0, 3)  2.87 us
  transfers between devices with their start and end apart: 8, of which 3 were waited for; matrix products, arithmetic and copies ran while one was open for 21% of the time, Pallas kernels for 0%

commit v1 on v0

v1 whole, which is shorter than its diff:
```python
import functools

import jax
import jax.numpy as jnp
from jax import lax
from jax.experimental import pallas as pl
from jax.experimental.pallas import tpu as pltpu
from jax.sharding import PartitionSpec as P

EPSILON = 1e-06
F32 = jnp.float32
BF16 = jnp.bfloat16
VMEM = pl.BlockSpec(memory_space=pltpu.VMEM)


def neighbours():
    return [(dz, dy) for dz in (-1, 0, 1) for dy in (-1, 0, 1) if (dz, dy) != (0, 0)]


def rim_kernel(n_gz, n_xy, block, framed, send, recv):
    depth, rows = block.shape[0], block.shape[1]
    gz, xy = lax.axis_index("gz"), lax.axis_index("xy")
    framed[...] = jnp.zeros_like(framed)
    framed[pl.ds(1, depth), pl.ds(1, rows)] = block[...]

    def there(dz, dy):
        inside = (gz + dz >= 0) & (gz + dz < n_gz) & (xy + dy >= 0) & (xy + dy < n_xy)
        return inside, (gz + dz, xy + dy)

    def span(step, size, far):
        if step == 0:
            return pl.ds(1, size) if far else pl.ds(0, size)
        if far:
            return pl.ds(0, 1) if step > 0 else pl.ds(size + 1, 1)
        return pl.ds(size - 1, 1) if step > 0 else pl.ds(0, 1)

    def copy(dz, dy, number):
        _, where = there(dz, dy)
        return pltpu.make_async_remote_copy(
            src_ref=block.at[span(dz, depth, False), span(dy, rows, False)],
            dst_ref=framed.at[span(dz, depth, True), span(dy, rows, True)],
            send_sem=send.at[number],
            recv_sem=recv.at[number],
            device_id=where,
            device_id_type=pl.DeviceIdType.MESH,
        )

    barrier = pltpu.get_barrier_semaphore()
    for dz, dy in neighbours():
        inside, where = there(dz, dy)

        @pl.when(inside)
        def _():
            pl.semaphore_signal(
                barrier, inc=1, device_id=where, device_id_type=pl.DeviceIdType.MESH
            )

    across = 1 + lax.min(gz, 1) + lax.min(n_gz - 1 - gz, 1)
    along = 1 + lax.min(xy, 1) + lax.min(n_xy - 1 - xy, 1)
    pl.semaphore_wait(barrier, across * along - 1)

    for number, (dz, dy) in enumerate(neighbours()):

        @pl.when(there(dz, dy)[0])
        def _():
            copy(dz, dy, number).start()

    for number, (dz, dy) in enumerate(neighbours()):

        @pl.when(there(dz, dy)[0])
        def _():
            copy(dz, dy, number).wait_send()

        @pl.when(there(-dz, -dy)[0])
        def _():
            copy(dz, dy, number).wait_recv()


def with_rims(block, collective_id, n_gz, n_xy):
    depth, rows, pairs, lanes = block.shape
    return pl.pallas_call(
        functools.partial(rim_kernel, n_gz, n_xy),
        out_shape=jax.ShapeDtypeStruct((depth + 2, rows + 2, pairs, lanes), block.dtype),
        in_specs=[VMEM],
        out_specs=VMEM,
        scratch_shapes=[pltpu.SemaphoreType.DMA((8,))] * 2,
        compiler_params=pltpu.CompilerParams(collective_id=collective_id, has_side_effects=True),
    )(block)


def weight_halves(weight, half, turned):
    lows, highs = [], []
    count = weight.shape[1] // half
    for first in range(0, count, 2):
        if first + 1 < count:
            near = weight[:, pl.ds(first * half, 2 * half)].astype(F32)
        else:
            last = weight[:, pl.ds(first * half, half)].astype(F32)
            near = jnp.concatenate([last, jnp.zeros_like(last)], axis=1)
        far = pltpu.roll(near, half, 1)
        if turned:
            both = jnp.concatenate([near, far], axis=0).T
            near, far = both[:half], both[half:]
        lows += [near, far]
        highs += [far, near]
    return lows, highs


def fill_band(target, weight, turned):
    half = weight.shape[0]
    lows, highs = weight_halves(weight, half, turned)
    low = lax.broadcasted_iota(jnp.int32, (half, 2 * half), 1) < half
    for offset in range(9):
        ks = [26 - 3 * offset - x if turned else 3 * offset + x for x in range(3)]
        parts = [
            jnp.where(low, lows[ks[1]], highs[ks[0]]),
            jnp.where(low, lows[ks[2]], highs[ks[1]]),
            jnp.where(low, 0.0, highs[ks[2]]),
            jnp.where(low, lows[ks[0]], 0.0),
        ]
        for place, part in enumerate(parts):
            target[pl.ds((4 * offset + place) * half, half), :] = part.astype(BF16)


def side_lanes(cells, half, period):
    pairs = cells.shape[1]
    lane = lax.broadcasted_iota(jnp.int32, cells.shape, 2)
    place = lax.broadcasted_iota(jnp.int32, cells.shape, 1) % period
    right = pltpu.roll(cells, pairs - 1, 1)
    left = pltpu.roll(cells, 1, 1)
    low = lane < half
    right = jnp.where(place == period - 1, 0.0, right)
    left = jnp.where(place == 0, 0.0, left)
    return jnp.where(low, right, left)


def fill_windows(target, source, half, period, inner):
    depth = target.shape[0]
    lanes = 2 * half
    if inner:
        target[...] = jnp.zeros_like(target)
    first, last = (1, depth - 1) if inner else (0, depth)
    for z in range(first, last):
        cells = source(z - first)
        rows = pl.ds(1, target.shape[1] - 2) if inner else pl.ds(0, target.shape[1])
        target[z, rows, :, pl.ds(0, lanes)] = cells.astype(BF16)
        target[z, rows, :, pl.ds(lanes, lanes)] = side_lanes(cells.astype(F32), half, period).astype(
            BF16
        )


def window_rows(windows, z, count, dz, dy):
    rows = windows.shape[1] - 2
    pairs, width = windows.shape[2], windows.shape[3]
    part = windows[pl.ds(z + dz, count), pl.ds(dy, rows)]
    return part.reshape(count * rows * pairs, width)


def conv_rows(windows, weight, z, count):
    parts = [window_rows(windows, z, count, dz, dy) for dz in range(3) for dy in range(3)]
    return jnp.dot(jnp.concatenate(parts, axis=1), weight[...], preferred_element_type=F32)


def outer_sums(out, base, windows, grad_turned, half):
    depth = windows.shape[0] - 2
    lanes = 2 * half
    lane = lax.broadcasted_iota(jnp.int32, (half, lanes), 1)
    held = None
    for offset in range(9):
        both = jnp.dot(
            grad_turned,
            window_rows(windows, 0, depth, offset // 3, offset % 3),
            preferred_element_type=F32,
        )
        top_near, top_far = both[:half, :lanes], both[:half, lanes:]
        far_turned = pltpu.roll(top_far, half, 1)
        near_turned = pltpu.roll(top_near, half, 1)
        first = jnp.where(lane < half, far_turned, near_turned) + both[half:, :lanes]
        third = near_turned + both[half:, lanes:]
        out[pl.ds(base + offset * half, half), :] = first.astype(BF16)
        if offset % 2 == 0:
            held = jnp.where(lane < half, third, 0.0)
        else:
            pair = held + jnp.where(lane < half, 0.0, pltpu.roll(third, half, 1))
            out[pl.ds(base + (9 + offset // 2) * half, half), :] = pair.astype(BF16)
    out[pl.ds(base + 13 * half, half), :] = held.astype(BF16)


def refine_kernel(
    period, vol, cot, back, refine, mix, fgrad, rsum, msum, xw, fw, pw, wb, wr, wrt, gate_s, pg_s
):
    depth, rows, pairs, lanes = fgrad.shape
    half = lanes // 2
    step = 4 if depth % 4 == 0 else depth
    flat = step * rows * pairs
    fill_band(wb, back, False)
    fill_band(wr, refine, False)
    fill_band(wrt, refine, True)
    mixed = mix[...].astype(F32)
    mixed = jnp.concatenate([mixed, jnp.zeros_like(mixed)], axis=1)
    mix2 = jnp.concatenate([mixed, pltpu.roll(mixed, half, 1)], axis=0).T.astype(BF16)
    fill_windows(xw, lambda z: vol[z], half, pairs, False)
    fw[...] = jnp.zeros_like(fw)
    pw[...] = jnp.zeros_like(pw)
    inner = pl.ds(1, rows)

    def put(target, z, cells):
        target[pl.ds(z + 1, step), inner, :, pl.ds(0, lanes)] = cells.astype(BF16)
        near = cells.astype(F32).reshape(step * rows, pairs, lanes)
        target[pl.ds(z + 1, step), inner, :, pl.ds(lanes, lanes)] = (
            side_lanes(near, half, period).astype(BF16).reshape(step, rows, pairs, lanes)
        )

    for z in range(0, depth, step):
        own = vol[pl.ds(z + 1, step), inner].astype(F32).reshape(flat, lanes)
        feature = (own + conv_rows(xw, wb, z, step)).astype(BF16)
        put(fw, z, feature.reshape(step, rows, pairs, lanes))
    for z in range(0, depth, step):
        pre = conv_rows(fw, wr, z, step)
        sig = jax.nn.sigmoid(pre)
        total = cot[pl.ds(z, step)].reshape(flat, lanes).astype(BF16)
        gate_s[pl.ds(z * rows * pairs, flat), :] = (pre * sig).astype(BF16)
        gated_grad = jnp.dot(total, mix2, preferred_element_type=F32)
        pre_grad = (gated_grad * sig * (1.0 + pre * (1.0 - sig))).astype(BF16)
        pg_s[pl.ds(z * rows * pairs, flat), :] = pre_grad
        put(pw, z, pre_grad.reshape(step, rows, pairs, lanes))
    for z in range(0, depth, step):
        total = cot[pl.ds(z, step)].reshape(flat, lanes)
        grad = total + conv_rows(pw, wrt, z, step)
        fgrad[pl.ds(z, step)] = grad.astype(BF16).reshape(step, rows, pairs, lanes)
    outer_sums(rsum, 0, fw, pg_s[...].T, half)
    cot_rows = cot[...].reshape(depth * rows * pairs, lanes).astype(BF16)
    both = jnp.dot(gate_s[...].T, cot_rows, preferred_element_type=F32)
    lane = lax.broadcasted_iota(jnp.int32, (half, lanes), 1)
    msum[...] = jnp.where(lane < half, both[:half] + pltpu.roll(both[half:], half, 1), 0.0).astype(
        BF16
    )


def backbone_kernel(vol, grad, back, rsum, msum, vgrad, sums, xw, gw, wbt):
    depth, rows, pairs, lanes = vgrad.shape
    half = lanes // 2
    step = 4 if depth % 4 == 0 else depth
    flat = step * rows * pairs
    fill_band(wbt, back, True)
    fill_windows(xw, lambda z: vol[z], half, pairs, False)
    fill_windows(gw, lambda z: grad[z], half, pairs, False)
    inner = pl.ds(1, rows)
    for z in range(0, depth, step):
        own = grad[pl.ds(z + 1, step), inner].astype(F32).reshape(flat, lanes)
        out = own + conv_rows(gw, wbt, z, step)
        vgrad[pl.ds(z, step)] = out.astype(BF16).reshape(step, rows, pairs, lanes)
    own = grad[pl.ds(1, depth), inner].reshape(depth * rows * pairs, lanes)
    outer_sums(sums, 0, xw, own.T, half)
    block = rsum.shape[0]
    sums[pl.ds(block, block), :] = rsum[...]
    sums[pl.ds(2 * block, half), :] = msum[...]
    used = 2 * block + half
    if used < sums.shape[0]:
        sums[pl.ds(used, sums.shape[0] - used), :] = jnp.zeros(
            (sums.shape[0] - used, lanes), BF16
        )


def total_kernel(n_gz, n_xy, sums, out, got1, part, got2, mine, *sems):
    gz, xy = lax.axis_index("gz"), lax.axis_index("xy")
    chunk = mine.shape[0]
    block = part.shape[0]
    barrier = pltpu.get_barrier_semaphore()

    def peer(axis, step):
        if axis == "gz":
            target = lax.rem(gz + step, n_gz)
            return target, (target, xy)
        target = lax.rem(xy + step, n_xy)
        return target, (gz, target)

    sizes = {"gz": n_gz, "xy": n_xy}

    def each(axis, action):
        def one(step, carry):
            action(step)
            return carry

        lax.fori_loop(1, sizes[axis], one, 0)

    def greet(axis):
        def one(step):
            pl.semaphore_signal(
                barrier,
                inc=1,
                device_id=peer(axis, step)[1],
                device_id_type=pl.DeviceIdType.MESH,
            )

        each(axis, one)

    greet("gz")
    greet("xy")
    pl.semaphore_wait(barrier, n_gz + n_xy - 2)

    def copy(axis, stage, source, target):
        def make(step):
            where, device = peer(axis, step)
            return pltpu.make_async_remote_copy(
                src_ref=source(where),
                dst_ref=target(step),
                send_sem=sems[2 * stage].at[step],
                recv_sem=sems[2 * stage + 1].at[step],
                device_id=device,
                device_id_type=pl.DeviceIdType.MESH,
            )

        return make

    blocks = copy("gz", 0, lambda w: sums.at[pl.ds(w * block, block)], lambda s: got1.at[s])
    each("gz", lambda step: blocks(step).start())
    each("gz", lambda step: blocks(step).wait_recv())
    total = sums[pl.ds(gz * block, block), :].astype(F32)
    for step in range(1, n_gz):
        total = total + got1[step].astype(F32)
    part[...] = total.astype(BF16)
    chunks = copy("xy", 1, lambda w: part.at[pl.ds(w * chunk, chunk)], lambda s: got2.at[s])
    each("xy", lambda step: chunks(step).start())
    each("xy", lambda step: chunks(step).wait_recv())
    total = part[pl.ds(xy * chunk, chunk), :].astype(F32)
    for step in range(1, n_xy):
        total = total + got2[step].astype(F32)
    mine[...] = total.astype(BF16)
    own = pl.ds(gz * block + xy * chunk, chunk)
    spread = copy("xy", 2, lambda w: mine, lambda s: out.at[own])
    each("xy", lambda step: spread(step).start())
    out[own, :] = mine[...]
    each("xy", lambda step: spread(step).wait_recv())
    ours = pl.ds(gz * block, block)
    again = copy("gz", 3, lambda w: out.at[ours], lambda s: out.at[ours])
    each("gz", lambda step: again(step).start())
    each("gz", lambda step: blocks(step).wait_send())
    each("xy", lambda step: chunks(step).wait_send())
    each("xy", lambda step: spread(step).wait_send())
    each("gz", lambda step: again(step).wait())


def finish_kernel(totals, back_step, refine_step, mix_step):
    half = mix_step.shape[0]
    lanes = 2 * half
    block = 14 * half
    low = lax.broadcasted_iota(jnp.int32, (half, lanes), 1) < half

    def scale_of(values, count):
        squares = jnp.sum(values * values, axis=0, keepdims=True)
        return jnp.sqrt(jnp.sum(squares, axis=1, keepdims=True) / count + EPSILON)

    for base, out in ((0, back_step), (block, refine_step)):
        values = totals[pl.ds(base, block), :].astype(F32)
        scale = scale_of(values, 27.0 * half * half)
        lows, highs = [None] * 28, [None] * 28
        for tile in range(14):
            near = values[tile * half : (tile + 1) * half]
            both = jnp.concatenate([near, pltpu.roll(near, half, 1)], axis=0).T / scale
            if tile < 9:
                first, second = 3 * tile, 3 * tile + 1
            else:
                first, second = 6 * (tile - 9) + 2, 6 * (tile - 9) + 5
            lows[first], highs[first] = both[:half], both[half:]
            if second < 27:
                lows[second], highs[second] = both[half:], both[:half]
        for k in range(0, 26, 2):
            out[:, pl.ds(k * half, lanes)] = jnp.where(low, lows[k], highs[k + 1])
        out[:, pl.ds(26 * half, half)] = lows[26][:, :half]
    values = totals[pl.ds(2 * block, half), :].astype(F32)
    mix_step[...] = (values / scale_of(values, 1.0 * half * half))[:, :half]


def body(volume, backbone_weight, refine_weight, mix_weight, tile_cot, tile_slot, tile_count):
    depth, rows, width = volume.shape
    channels = mix_weight.shape[0]
    edge = tile_cot.shape[4]
    owners, capacity = tile_cot.shape[2], tile_cot.shape[3]
    assert depth == edge and rows == edge
    lanes = 2 * channels
    pairs = width // lanes
    period = edge // 2
    tiles = pairs // period
    slots = owners * capacity
    n_gz, n_xy = lax.axis_size("gz"), lax.axis_size("xy")
    devices = n_gz * n_xy
    brick = (depth, rows, pairs, lanes)
    rimmed = with_rims(volume.reshape(brick), 1, n_gz, n_xy)

    my_counts = jnp.sum(
        tile_count[0]
        * (jnp.arange(owners, dtype=jnp.int32) == lax.axis_index("xy")).astype(jnp.int32)[:, None],
        axis=0,
    )
    live = (jnp.arange(capacity, dtype=jnp.int32)[None, :] < my_counts[:, None]).reshape(slots)
    picker = (
        (tile_slot.reshape(slots)[None, :] == jnp.arange(tiles, dtype=jnp.int32)[:, None])
        & live[None, :]
    ).astype(BF16)
    cot = jnp.dot(
        picker, tile_cot.reshape(slots, edge * edge * edge * channels), preferred_element_type=F32
    )
    cot = cot.reshape(tiles, depth, rows, period, lanes).transpose(1, 2, 0, 3, 4).reshape(brick)

    block = 14 * channels
    framed = (depth + 2, rows + 2, pairs, 2 * lanes)
    params = pltpu.CompilerParams(vmem_limit_bytes=56 * 1024 * 1024)
    fgrad, rsum, msum = pl.pallas_call(
        functools.partial(refine_kernel, period),
        out_shape=(
            jax.ShapeDtypeStruct(brick, BF16),
            jax.ShapeDtypeStruct((block, lanes), BF16),
            jax.ShapeDtypeStruct((channels, lanes), BF16),
        ),
        in_specs=[VMEM] * 5,
        out_specs=(VMEM,) * 3,
        scratch_shapes=[
            pltpu.VMEM(framed, BF16),
            pltpu.VMEM(framed, BF16),
            pltpu.VMEM(framed, BF16),
            pltpu.VMEM((36 * channels, lanes), BF16),
            pltpu.VMEM((36 * channels, lanes), BF16),
            pltpu.VMEM((36 * channels, lanes), BF16),
            pltpu.VMEM((depth * rows * pairs, lanes), BF16),
            pltpu.VMEM((depth * rows * pairs, lanes), BF16),
        ],
        compiler_params=params,
    )(
        rimmed,
        cot,
        backbone_weight,
        refine_weight,
        mix_weight,
    )
    grad_rimmed = with_rims(fgrad, 2, n_gz, n_xy)
    used = 2 * block + channels
    chunk = -(-used // (devices * 16)) * 16
    vgrad, sums = pl.pallas_call(
        backbone_kernel,
        out_shape=(
            jax.ShapeDtypeStruct(brick, BF16),
            jax.ShapeDtypeStruct((devices * chunk, lanes), BF16),
        ),
        in_specs=[VMEM] * 5,
        out_specs=(VMEM,) * 2,
        scratch_shapes=[
            pltpu.VMEM(framed, BF16),
            pltpu.VMEM(framed, BF16),
            pltpu.VMEM((36 * channels, lanes), BF16),
        ],
        compiler_params=params,
    )(rimmed, grad_rimmed, backbone_weight, rsum, msum)
    totals = pl.pallas_call(
        functools.partial(total_kernel, n_gz, n_xy),
        out_shape=jax.ShapeDtypeStruct((devices * chunk, lanes), BF16),
        in_specs=[VMEM],
        out_specs=VMEM,
        scratch_shapes=[
            pltpu.VMEM((n_gz, n_xy * chunk, lanes), BF16),
            pltpu.VMEM((n_xy * chunk, lanes), BF16),
            pltpu.VMEM((n_xy, chunk, lanes), BF16),
            pltpu.VMEM((chunk, lanes), BF16),
        ]
        + [pltpu.SemaphoreType.DMA((n,)) for n in (n_gz, n_gz, n_xy, n_xy, n_xy, n_xy, n_gz, n_gz)],
        compiler_params=pltpu.CompilerParams(collective_id=0, has_side_effects=True),
    )(sums)
    wide = jax.ShapeDtypeStruct((channels, 27 * channels), F32)
    back_step, refine_step, mix_step = pl.pallas_call(
        finish_kernel,
        out_shape=(wide, wide, jax.ShapeDtypeStruct((channels, channels), F32)),
        in_specs=[VMEM],
        out_specs=(VMEM,) * 3,
    )(totals)
    return (vgrad.reshape(depth, rows, width), back_step, refine_step, mix_step)


def solution(mesh):
    in_specs = (
        P("gz", "xy", None),
        P(),
        P(),
        P(),
        P("gz", "xy", None, None, None, None, None),
        P("gz", "xy", None, None),
        P("gz", None, None),
    )
    out_specs = (P("gz", "xy", None), P(), P(), P())
    return jax.shard_map(body, mesh=mesh, in_specs=in_specs, out_specs=out_specs, check_vma=False)
```

time: 122 us -> 65.4 us (0.54)
  local copies, waits for them, and re-layouts: 36.1 us -> 5.8 us
  starting transfers between devices: 20.7 us -> 0 us
  Pallas kernels: 50.6 us -> 57.3 us
  other arithmetic: 6.55 us -> 0.16 us
  waiting for transfers between devices: 5.55 us -> 0 us
    ppermute x8 -> x0, starting transfers between devices: 20.7 us -> none  [the longest x4 15.6 us: with_rims(): lax.ppermute(lax.slice_in_dim(block, size - 1, None, axis=dim), axis, for...]
    slice x20 -> x0, local copies, waits for them, and re-layouts: 17.6 us -> none  [the longest x9 11.2 us: banded(): w0, w1, w2 = (blocks[:, 0], blocks[:, 1], blocks[:, 2])]
    reshape x16 -> x1, local copies, waits for them, and re-layouts: 10.4 us -> 0.82 us  [body(): return (vgrad.reshape(depth, rows, width), back_step, refine_step, mix_step)]
    pallas_call x1 -> x4, Pallas kernels: 38.9 us -> 45.8 us  [the longest x1 26.7 us: body(): pl.pallas_call(functools.partial(total_kernel, n_gz, n_xy), out_shape=jax...]
    concatenate x7 -> x0, other arithmetic: 6.38 us -> none  [the longest x2 3.27 us: banded(): both = jnp.concatenate([left, right], axis=2)]
    ppermute x8 -> x0, waiting for transfers between devices: 5.55 us -> none  [the longest x4 2.79 us: with_rims(): high = lax.ppermute(lax.slice_in_dim(block, 0, 1, axis=dim), axis, backward)]
    unnamed x30 -> x10, local copies, waits for them, and re-layouts: 2.46 us -> 2.57 us
  transfers between devices with their start and end apart: 8 -> 0, of which waited for: 3 -> 0; matrix products, arithmetic and copies ran while one was open for 21% -> 0% of each run, Pallas kernels for 0% -> 0%
where the time goes in v1:
time: 65.4 us; the launch traced here: 64.6 us
  Pallas kernels  57.3 us (88%)
  local copies, waits for them, and re-layouts  5.8 us (9%)
  between operations  0.72 us (1%)
  matrix products  0.68 us (1%)
    pallas_call x1, Pallas kernels, body(): pl.pallas_call(functools.partial(total_kernel, n_gz, n_xy), out_shape=jax...  26.7 us
    pallas_call x2, Pallas kernels, with_rims(): pl.pallas_call(functools.partial(rim_kernel, n_gz, n_xy), out_shape=jax.S...  16.4 us
    pallas_call x1, Pallas kernels, body(): pl.pallas_call(functools.partial(refine_kernel, period), out_shape=(jax.S...  7 us
    pallas_call x1, Pallas kernels, body(): pl.pallas_call(backbone_kernel, out_shape=(jax.ShapeDtypeStruct(brick, BF...  4.48 us
    pallas_call x1, Pallas kernels, body(): pl.pallas_call(finish_kernel, out_shape=(wide, wide, jax.ShapeDtypeStruct...  2.68 us
    unnamed x10, local copies, waits for them, and re-layouts  2.57 us

profile of v1, /device:TPU:0, one launch (start us, length us, event | category | flops | bytes accessed | tf_op | source)
XLA Modules:
  0.0 64.6 jit_solution(15769973267139156681)
XLA Ops:
  0.6 0.0 copy-start
  0.6 1.8 %copy.21 = bf16[8,8,16,128]{3,2,1,0:T(8,128)(2,1)} copy(bf16[8,8,16,128]{3,1,2,0:T(8,128)(2,1)} %bitcast.29) | data formatting | bytes 524288
  2.4 8.4 %shard_map.102.vol = bf16[10,10,16,128]{3,2,1,0:T(8,128)(2,1)} custom-call(bf16[8,8,16,128]{3,2,1,0:T(8,128)(2,1)} %copy.21), custom_call_target="tpu_custom_call" | custom-call | tf_op jit(solution)/shard_map/pallas_call | solution.py:81
  10.9 0.0 copy-done
  10.9 0.5 reshape.44
  11.4 0.0 copy-start.3
  11.4 0.8 %dot_general.8 = bf16[8,8,4,128,16]{3,2,1,0,4:T(4,128)(2,1)S(1)} reshape(bf16[32768,16]{0,1:T(8,128)(2,1)S(1)} %bitcast.27) | data formatting | bytes 2097152 | tf_op jit(solution)/shard_map/dot_general | solution.py:401
  12.2 0.0 copy-done.3
  12.2 0.1 copy.13
  12.3 0.1 eq.25
  12.4 0.7 %copy-done.2 = s32[1,8,8]{2,1,0:T(8,128)S(1)} copy-done((s32[1,8,8]{2,1,0:T(8,128)S(1)}, s32[1,8,8]{2,1,0:T(8,128)}, u32[]{:S(2)}) %copy-start.2) | copy-done | bytes 280
  13.1 0.1 fusion.1
  13.2 0.1 iota_compare_fusion
  13.2 0.1 lt.23
  13.3 0.7 %convolution_bitcast_fusion = f32[8,8,4,4,128]{4,2,3,1,0:T(4,128)S(1)} fusion(bf16[8,8,4,128,16]{3,2,1,0,4:T(4,128)(2,1)S(1)} %dot_general.8, s32[16]{0:T(128)S(1)} %eq.25, pred[16]{0:T(512)(128)(4,1)S(1)} %lt.23), kind=kOutput, calls=%fused_computation | convolution fusion | flops 4194432 | bytes 1572944 | tf_op jit(solution)/shard_map/dot_general | solution.py:401
  14.0 0.9 %copy.15 = f32[8,8,4,4,128]{4,3,2,1,0:T(4,128)} copy(f32[8,8,4,4,128]{4,2,3,1,0:T(4,128)S(1)} %convolution_bitcast_fusion) | data formatting | bytes 1048576 | tf_op jit(solution)/shard_map/transpose | solution.py:404
  14.9 7.0 %shard_map.103 = (bf16[8,8,16,128]{3,2,1,0:T(8,128)(2,1)}, bf16[896,128]{1,0:T(8,128)(2,1)}, bf16[64,128]{1,0:T(8,128)(2,1)}) custom-call(bf16[10,10,16,128]{3,2,1,0:T(8,128)(2,1)} %shard_map.102.vol, f32[8,8,16,128]{3,2,1,0:T(8,128)} %bitcast.28, bf16[64,1728]{1,0:T(8,128)(2,1)} %back.3, bf16[64,1728]{1,0:T(8,128)(2,1)} %refine.1, bf16[64,64]{1,0:T(8,128)(2,1)} %mix.1), custom_call_target="tpu_custom_call" | custom-call | tf_op jit(solution)/shard_map/pallas_call | solution.py:409
  21.9 8.0 %shard_map.104.grad = bf16[10,10,16,128]{3,2,1,0:T(8,128)(2,1)} custom-call(bf16[8,8,16,128]{3,2,1,0:T(8,128)(2,1)} %get-tuple-element.12.block), custom_call_target="tpu_custom_call" | custom-call | tf_op jit(solution)/shard_map/pallas_call | solution.py:81
  29.9 4.5 %shard_map.105 = (bf16[8,8,16,128]{3,2,1,0:T(8,128)(2,1)}, bf16[2048,128]{1,0:T(8,128)(2,1)}) custom-call(bf16[10,10,16,128]{3,2,1,0:T(8,128)(2,1)} %shard_map.102.vol, bf16[10,10,16,128]{3,2,1,0:T(8,128)(2,1)} %shard_map.104.grad, bf16[64,1728]{1,0:T(8,128)(2,1)} %back.3, bf16[896,128]{1,0:T(8,128)(2,1)} %get-tuple-element.13.rsum, ...), custom_call_target="tpu_custom_call" | custom-call | tf_op jit(solution)/shard_map/pallas_call | solution.py:439
  34.4 26.7 %shard_map.106.totals = bf16[2048,128]{1,0:T(8,128)(2,1)} custom-call(bf16[2048,128]{1,0:T(8,128)(2,1)} %get-tuple-element.16.sums), custom_call_target="tpu_custom_call" | custom-call | tf_op jit(solution)/shard_map/pallas_call | solution.py:454
  61.1 0.0 copy-start.1
  61.1 2.7 %shard_map.107 = (f32[64,1728]{1,0:T(8,128)}, f32[64,1728]{1,0:T(8,128)}, f32[64,64]{1,0:T(8,128)}) custom-call(bf16[2048,128]{1,0:T(8,128)(2,1)} %shard_map.106.totals), custom_call_target="tpu_custom_call" | custom-call | tf_op jit(solution)/shard_map/pallas_call | solution.py:469
  63.8 0.0 copy-done.1
  63.8 0.8 %reshape.46 = bf16[8,8,2048]{2,1,0:T(8,128)(2,1)} reshape(bf16[8,8,16,128]{3,2,1,0:T(8,128)(2,1)S(1)} %copy-done.1) | data formatting | bytes 524288 | tf_op jit(solution)/shard_map/reshape | solution.py:475
  (2 shorter events, 0.0 us)
Async XLA Ops:
  0.6 10.2 %copy-start = (bf16[1,1,8,2,8,8,512]{6,5,4,3,2,1,0:T(8,128)(2,1)S(1)}, bf16[1,1,8,2,8,8,512]{6,5,4,3,2,1,0:T(8,128)(2,1)}, u32[]{:S(2)}) copy-start(bf16[1,1,8,2,8,8,512]{6,5,4,3,2,1,0:T(8,128)(2,1)} %param.11) | copy-start | bytes 3145732
  11.4 0.8 %copy-start.3 = (s32[1,1,8,2]{2,3,1,0:T(2,128)S(1)}, s32[1,1,8,2]{2,3,1,0:T(2,128)}, u32[]{:S(2)}) copy-start(s32[1,1,8,2]{2,3,1,0:T(2,128)} %param.12) | copy-start | bytes 196
  12.4 0.7 %copy-start.2 = (s32[1,8,8]{2,1,0:T(8,128)S(1)}, s32[1,8,8]{2,1,0:T(8,128)}, u32[]{:S(2)}) copy-start(s32[1,8,8]{2,1,0:T(8,128)} %param.13) | copy-start | bytes 772
  61.1 2.7 %copy-start.1 = (bf16[8,8,16,128]{3,2,1,0:T(8,128)(2,1)S(1)}, bf16[8,8,16,128]{3,2,1,0:T(8,128)(2,1)}, u32[]{:S(2)}) copy-start(bf16[8,8,16,128]{3,2,1,0:T(8,128)(2,1)} %get-tuple-element.15) | copy-start | bytes 786436
